TPU v7x, 32 devices: a whole 2x2x4 slice. The times are simulated.
32 devices in a mesh: groups: 2 (over y), row: 16 (over z, x, core).
Axes of the slice: x: 2, y: 2, z: 4, core: 2. Of those that a mesh axis runs over, the one named last changes fastest.
Arguments:
- homolog_activation: float32 [32, 512, 256], P('groups', 'row'), parts along dimension 0, may hold values from -6 to 6
- homolog_entry_valid: int32 [32, 512], P('groups', 'row'), parts along dimension 0, may hold values 0 or 1
- amino_valid_flags: int32 [1024], P(('groups', 'row')), parts along dimension 0, may hold values 0 or 1
- first_factor_weights: float32 [256, 32], replicated, may hold values from -0.375 to 0.375
- second_factor_weights: float32 [256, 32], replicated, may hold values from -0.375 to 0.375
- final_linear_weights: float32 [1024, 128], replicated, may hold values from -0.1875 to 0.1875
- couple_delta_deriv: float32 [1024, 512, 128], P(('groups', 'row')), parts along dimension 0, may hold values from -6 to 6
Outputs:
- alignment_grad: float32 [32, 512, 256], P('groups', 'row'), parts along dimension 0
- left_weight_grad: float32 [512, 32], P('groups'), parts along dimension 0
- right_weight_grad: float32 [512, 32], P('groups'), parts along dimension 0
- out_weight_grad: float32 [2048, 128], P('groups'), parts along dimension 0
There are 2 independent parts, one for each index of `groups`. A program takes and returns all parts, laid end to end along the dimension named above; an argument that names none is the same for every part. Nothing has to cross between parts.
All inputs are finite; a program needn't handle non-finite values. No bound on the sum of `homolog_entry_valid` or of `amino_valid_flags` on one device may be relied on, other than what follows from the above.
Results may differ from a plain program's by a relative error of at most 0.0003.
Values sent between devices are 32-bit elements; how exact they have to be, the bound alone decides.
A program may use at most 128 MiB of HBM per device.

v0:
```python
import jax
import jax.numpy as jnp
from jax import lax
from jax.sharding import PartitionSpec as P

SPLIT_PIECES = lax.Precision.HIGHEST


def local(
    homolog_activation,
    homolog_entry_valid,
    amino_valid_flags,
    first_factor_weights,
    second_factor_weights,
    final_linear_weights,
    couple_delta_deriv,
):
    rows = couple_delta_deriv.shape[0]
    total = couple_delta_deriv.shape[1]
    homolog_number_here = homolog_activation.shape[0]
    width = first_factor_weights.shape[1]
    pair_width = final_linear_weights.shape[1]
    keep_mask = homolog_entry_valid.astype(jnp.float32).T
    present = amino_valid_flags.astype(jnp.float32)
    homolog_slice_here = jnp.transpose(homolog_activation, (1, 0, 2))
    first_factor_embed = (
        jnp.einsum("plg,gz->plz", homolog_slice_here, first_factor_weights, precision=SPLIT_PIECES)
        * keep_mask[:, :, None]
    )
    second_factor_embed = (
        jnp.einsum("plg,gz->plz", homolog_slice_here, second_factor_weights, precision=SPLIT_PIECES)
        * keep_mask[:, :, None]
    )
    right_flat, keep_all, present_all = (
        lax.all_gather(
            second_factor_embed.reshape(rows, homolog_number_here * width),
            "row",
            axis=0,
            tiled=True,
        ),
        lax.all_gather(keep_mask, "row", axis=0, tiled=True),
        lax.all_gather(present, "row", axis=0, tiled=True),
    )
    right_all = right_flat.reshape(total, homolog_number_here, width)
    count = jnp.dot(
        keep_mask, keep_all.T, precision=SPLIT_PIECES, preferred_element_type=jnp.float32
    )
    factor = present[:, None] * present_all[None, :] / jnp.maximum(count, 1.0)
    scaled = couple_delta_deriv * factor[:, :, None]
    w_three = final_linear_weights.reshape(width, width, pair_width)
    block = min(256, total)
    right_pieces = []
    for begin in range(0, total, block):
        piece = scaled[:, begin : begin + block]
        feats = jnp.einsum("rjk,abk->rjab", piece, w_three, precision=SPLIT_PIECES)
        right_pieces.append(
            jnp.einsum("rjab,rsa->jsb", feats, first_factor_embed, precision=SPLIT_PIECES)
        )
    carried = jnp.einsum("rjk,jsc->rsck", scaled, right_all, precision=SPLIT_PIECES)
    output_grad = jnp.einsum("rsa,rsck->ack", first_factor_embed, carried, precision=SPLIT_PIECES)
    first_factor_embed_deriv = jnp.einsum("rsck,ack->rsa", carried, w_three, precision=SPLIT_PIECES)
    right_terms = jnp.concatenate(right_pieces, axis=0)
    summed = lax.psum(right_terms, "row")
    second_factor_embed_deriv = lax.dynamic_slice_in_dim(
        summed, lax.axis_index("row") * rows, rows, 0
    )
    first_factor_embed_deriv = first_factor_embed_deriv * keep_mask[:, :, None]
    second_factor_embed_deriv = second_factor_embed_deriv * keep_mask[:, :, None]
    alignment_grad = jnp.einsum(
        "gyo,fo->ygf", first_factor_embed_deriv, first_factor_weights, precision=SPLIT_PIECES
    ) + jnp.einsum(
        "gyo,fo->ygf", second_factor_embed_deriv, second_factor_weights, precision=SPLIT_PIECES
    )
    first_operand_array = jnp.einsum(
        "dxb,dxo->bo", homolog_slice_here, first_factor_embed_deriv, precision=SPLIT_PIECES
    )
    second_operand_array = jnp.einsum(
        "dxb,dxo->bo", homolog_slice_here, second_factor_embed_deriv, precision=SPLIT_PIECES
    )
    output_grad_total, left_grad_total, right_grad_total = lax.psum(
        (output_grad.reshape(width * width, pair_width), first_operand_array, second_operand_array),
        "row",
    )
    return (alignment_grad, left_grad_total, right_grad_total, output_grad_total)


def solution(mesh):
    in_specs = (
        P("groups", "row", None),
        P("groups", "row"),
        P(("groups", "row")),
        P(),
        P(),
        P(),
        P(("groups", "row"), None, None),
    )
    out_specs = (P("groups", "row", None), P("groups", None), P("groups", None), P("groups", None))
    return jax.shard_map(local, mesh=mesh, in_specs=in_specs, out_specs=out_specs, check_vma=False)
```

profile of v0, /device:TPU:0, one launch (start us, length us, event | category | flops | bytes accessed | tf_op | source)
XLA Modules:
  0.0 452.7 jit_solution(17768828914577271759)
XLA Ops:
  8.0 1.8 convolution_multiply_fusion.1
  10.7 23.5 %all-gather = f32[16,32,16]{1,2,0:T(8,128)S(1)} all-gather(f32[1,32,16]{1,2,0:T(8,128)S(1)} %get-tuple-element.24), channel_id=1, replica_groups=mesh['groups'=2,'row'=16] {'row'}, dimensions={0}, use_global_device_ids=true | all-gather | bytes 34816 | tf_op jit(solution)/shard_map/all_gather | solution.py:41
  37.6 29.9 %all-reduce = f32[512]{0:T(512)S(1)} all-reduce(f32[512]{0:T(512)S(1)} %convert_dynamic-update-slice_fusion), channel_id=1, replica_groups=mesh['groups'=2,'row'=16] {'row'}, use_global_device_ids=true, to_apply=%add | all-reduce | flops 512 | bytes 4096
  68.5 5.3 %broadcast_multiply_fusion = f32[32,512,128]{2,1,0:T(8,128)S(1)} fusion(f32[32,512,128]{2,1,0:T(8,128)} %param.13, f32[32,512]{1,0:T(8,128)S(1)} %fusion.22), kind=kLoop, calls=%fused_computation.11 | loop fusion | flops 2097152 | bytes 16842752 | tf_op jit(solution)/shard_map/mul | solution.py:49
  73.8 30.6 %fusion.7 = f32[32,256,32,32]{1,2,0,3:T(8,128)} fusion(f32[32,512,128]{2,1,0:T(8,128)S(1)} %broadcast_multiply_fusion, f32[32,32,128,1]{2,1,0,3:T(8,128)S(1)} %bitcast.87), kind=kOutput, calls=%fused_computation.9 | convolution fusion | flops 12884901888 | bytes 38273024 | tf_op jit(solution)/shard_map/rjk,abk->rjab/dot_general | solution.py:55
  104.5 31.1 %fusion.6 = f32[32,256,32,32]{1,2,0,3:T(8,128)} fusion(f32[32,512,128]{2,1,0:T(8,128)S(1)} %broadcast_multiply_fusion, f32[32,32,128,1]{2,1,0,3:T(8,128)S(1)} %bitcast.88), kind=kOutput, calls=%fused_computation.7 | convolution fusion | flops 12884901888 | bytes 38273024 | tf_op jit(solution)/shard_map/rjk,abk->rjab/dot_general | solution.py:55
  136.3 29.3 %convolution_bitcast_fusion.1 = f32[16,256,32]{1,0,2:T(8,128)} fusion(f32[32,16,32,1]{2,1,0,3:T(8,128)S(1)} %fusion.18, f32[32,256,32,32]{1,2,0,3:T(8,128)} %fusion.7), kind=kOutput, calls=%fused_computation.14 | convolution fusion | flops 1610612736 | bytes 34144256 | tf_op jit(solution)/shard_map/rjab,rsa->jsb/dot_general | solution.py:57
  165.7 2.4 copy.68
  168.1 29.5 %convolution_bitcast_fusion = f32[16,256,32]{1,0,2:T(8,128)} fusion(f32[32,16,32,1]{2,1,0,3:T(8,128)S(1)} %fusion.18, f32[32,256,32,32]{1,2,0,3:T(8,128)} %fusion.6), kind=kOutput, calls=%fused_computation.13 | convolution fusion | flops 1610612736 | bytes 34144256 | tf_op jit(solution)/shard_map/rjab,rsa->jsb/dot_general | solution.py:57
  197.6 3.6 copy.70
  201.2 3.8 pad_maximum_fusion
  205.0 1.6 copy.62
  206.6 16.1 %fusion.8 = f32[32,16,32,128]{3,2,0,1:T(8,128)S(1)} fusion(f32[512,16,32,1]{0,2,3,1:T(8,128)S(1)} %bitcast.91, f32[32,512,128]{2,1,0:T(8,128)} %copy-done.2), kind=kOutput, calls=%fused_computation.12 | convolution fusion | flops 12884901888 | bytes 17825792 | tf_op jit(solution)/shard_map/rjk,jsc->rsck/dot_general | solution.py:59
  222.7 3.2 copy-done.1
  226.0 9.4 %fusion.11 = f32[32,32,128]{2,0,1:T(8,128)S(1)} fusion(f32[32,16,32,1]{2,1,0,3:T(8,128)S(1)} %fusion.18, f32[32,16,32,128]{3,2,0,1:T(8,128)S(1)} %fusion.8), kind=kOutput, calls=%fused_computation.15 | convolution fusion | flops 805306368 | bytes 8978432 | tf_op jit(solution)/shard_map/rsa,rsck->ack/dot_general | solution.py:60
  236.6 14.4 %fusion.19 = f32[32,16,32]{2,1,0:T(8,128)S(1)} fusion(f32[32,16,32,128]{3,2,0,1:T(8,128)} %copy-done.1, f32[32,32,128]{2,1,0:T(8,128)S(1)} %bitcast.89, f32[32,16]{1,0:T(8,128)S(1)} %copy.61), kind=kOutput, calls=%fused_computation.22 | convolution fusion | flops 805322752 | bytes 8980480 | tf_op jit(solution)/shard_map/rsck,ack->rsa/dot_general | solution.py:61
  250.9 1.4 convolution_bitcast_fusion.3
  252.9 97.9 %all-reduce.8.cloned.1.call-done = (f32[512,16,32]{2,1,0:T(8,128)}, f32[1024,128]{1,0:T(8,128)}) async-done(((f32[512,16,32]{2,1,0:T(8,128)}, f32[1024,128]{1,0:T(8,128)}), (f32[512,16,32]{2,1,0:T(8,128)}, f32[1024,128]{1,0:T(8,128)})) %all-reduce.8.cloned.1.call-update) | async-done | bytes 1572880 | tf_op jit(solution)/shard_map/psum | solution.py:63
  350.8 2.4 convolution_bitcast_fusion.2
  353.3 1.6 fusion.14
  356.0 85.2 %all-reduce.6.cloned.1.call-done = (f32[256,32]{0,1:T(8,128)}, f32[256,32]{0,1:T(8,128)}) async-done(((f32[256,32]{0,1:T(8,128)}, f32[256,32]{0,1:T(8,128)}), (f32[256,32]{0,1:T(8,128)}, f32[256,32]{0,1:T(8,128)})) %all-reduce.6.cloned.1.call-update) | async-done | bytes 65552 | tf_op jit(solution)/shard_map/psum | solution.py:80
  441.2 1.4 copy.115
  442.6 1.4 copy.116
  444.0 1.9 copy.117
  (32 shorter events, 9.0 us)
Async XLA Ops:
  7.2 128.4 %copy-start = (f32[256,32]{0,1:T(8,128)S(1)}, f32[256,32]{0,1:T(8,128)}, u32[]{:S(2)}) copy-start(f32[256,32]{0,1:T(8,128)} %param.10) | copy-start | bytes 98308
  7.2 197.9 %all-gather.3.cloned.1.call-start = ((), (), s32[]{:S(2)}) async-start(), calls=%async_computation | async-start | bytes 1114112 | tf_op jit(solution)/shard_map/all_gather | solution.py:35
  10.6 340.2 %all-reduce.8.cloned.1.call-start = ((), (), s32[]{:S(2)}) async-start(), calls=%async_computation.2 | async-start | bytes 9437184 | tf_op jit(solution)/shard_map/psum | solution.py:63
  68.5 5.3 %copy-start.4 = (f32[1024,128]{1,0:T(8,128)S(1)}, f32[1024,128]{1,0:T(8,128)}, u32[]{:S(2)}) copy-start(f32[1024,128]{1,0:T(8,128)} %param.12) | copy-start | bytes 1572868
  73.8 30.7 %copy-start.2 = (f32[32,512,128]{2,1,0:T(8,128)}, f32[32,512,128]{2,1,0:T(8,128)S(1)}, u32[]{:S(2)}) copy-start(f32[32,512,128]{2,1,0:T(8,128)S(1)} %broadcast_multiply_fusion) | copy-start | bytes 25165828
  104.5 31.1 %copy-start.3 = (f32[16,32,256]{2,1,0:T(8,128)S(1)}, f32[16,32,256]{2,1,0:T(8,128)}, u32[]{:S(2)}) copy-start(f32[16,32,256]{2,1,0:T(8,128)} %param.7) | copy-start | bytes 1572868
  222.7 3.2 copy-start.1
  236.5 116.8 %copy-start.5 = (f32[256,32]{0,1:T(8,128)S(1)}, f32[256,32]{0,1:T(8,128)}, u32[]{:S(2)}) copy-start(f32[256,32]{0,1:T(8,128)} %param.11) | copy-start | bytes 98308
  236.5 204.7 %all-reduce.6.cloned.1.call-start = ((), (), s32[]{:S(2)}) async-start(), calls=%async_computation.1 | async-start | bytes 131072 | tf_op jit(solution)/shard_map/psum | solution.py:80
Sparse Core Ops, SparseCore 0:
  10.8 40.7 all-gather.2
  236.7 114.1 all-reduce.7
  355.0 86.2 all-reduce.5
where the time goes:
time: 461 us; the launch traced here: 453 us
  waiting for transfers between devices  183 us (40%)
  matrix products  170 us (37%)
  blocking collectives  53.4 us (12%)
  local copies, waits for them, and re-layouts  19.9 us (4%)
  between operations  14.8 us (3%)
  other arithmetic  11.2 us (2%)
    psum x1, waiting for transfers between devices, local(): summed = lax.psum(right_terms, 'row')  97.9 us
    psum x1, waiting for transfers between devices, local(): lax.psum((output_grad.reshape(width * width, pair_width), first_operand_a...  85.2 us
    dot_general x2, matrix products, local(): feats = jnp.einsum('rjk,abk->rjab', piece, w_three, precision=SPLIT_PIECES)  61.7 us
    dot_general x2, matrix products, local(): jnp.einsum('rjab,rsa->jsb', feats, first_factor_embed, precision=SPLIT_PI...  58.8 us
    unnamed x1, blocking collectives  29.9 us
    all_gather x1, blocking collectives, local(): lax.all_gather(keep_mask, 'row', axis=0, tiled=True)  23.5 us
    dot_general x1, matrix products, local(): jnp.einsum('rjk,jsc->rsck', scaled, right_all, precision=SPLIT_PIECES)  16.1 us
    dot_general x1, matrix products, local(): jnp.einsum('rsck,ack->rsa', carried, w_three, precision=SPLIT_PIECES)  14.4 us
  transfers between devices with their start and end apart: 3, of which 2 were waited for; matrix products, arithmetic and copies ran while one was open for 35% of the time, Pallas kernels for 0%

commit v1 on v0

v1 whole, which is shorter than its diff:
```python
import functools

import jax
import jax.numpy as jnp
from jax import lax
from jax.experimental import pallas as pl
from jax.experimental.pallas import tpu as pltpu
from jax.sharding import PartitionSpec as P

EXACT = lax.Precision.HIGHEST
F32, BF16 = jnp.float32, jnp.bfloat16
LANES = 128


def split(x):
    hi = x.astype(BF16)
    return hi, (x - hi.astype(F32)).astype(BF16)


def nn(a, b):
    return jnp.dot(a, b, preferred_element_type=F32)


def nt(a, b):
    return lax.dot_general(a, b, (((1,), (1,)), ((), ())), preferred_element_type=F32)


def remote(src, dst, send, recv, target):
    return pltpu.make_async_remote_copy(
        src_ref=src,
        dst_ref=dst,
        send_sem=send,
        recv_sem=recv,
        device_id={"row": target},
        device_id_type=pl.DeviceIdType.MESH,
    )


def places(n):
    me = lax.axis_index("row")
    return me, me + 1 - 2 * lax.rem(me, 2)


def greet(n):
    me, partner = places(n)
    barrier = pltpu.get_barrier_semaphore()
    pl.semaphore_signal(barrier, inc=1, device_id={"row": partner}, device_id_type=pl.DeviceIdType.MESH)

    def one(k, _):
        pl.semaphore_signal(
            barrier, inc=1, device_id={"row": lax.rem(me + 2 * k, n)}, device_id_type=pl.DeviceIdType.MESH
        )
        return 0

    lax.fori_loop(1, n // 2, one, 0)
    pl.semaphore_wait(barrier, n // 2)


def gather(n, own, out, send, fwd, recv):
    me, partner = places(n)
    half = n // 2

    def push(k, _):
        remote(own, out.at[me], send.at[k], recv.at[me], lax.rem(me + 2 * k, n)).start()
        return 0

    lax.fori_loop(1, half, push, 0)
    remote(own, out.at[me], send.at[0], recv.at[me], partner).start()
    out[me] = own[...]

    def relay(k, _):
        source = lax.rem(me - 2 * k + n, n)
        copy = remote(out.at[source], out.at[source], fwd.at[k], recv.at[source], partner)
        copy.wait_recv()
        copy.start()
        return 0

    lax.fori_loop(1, half, relay, 0)

    def arrive(k, _):
        source = lax.rem(partner - 2 * k + n, n)
        remote(own, out.at[source], send.at[k], recv.at[source], partner).wait_recv()
        return 0

    lax.fori_loop(0, half, arrive, 0)
    remote(own, out.at[me], send.at[0], recv.at[me], partner).wait_send()

    def sent(k, _):
        remote(own, out.at[me], send.at[k], recv.at[me], partner).wait_send()
        remote(own, out.at[me], fwd.at[k], recv.at[me], partner).wait_send()
        return 0

    lax.fori_loop(1, half, sent, 0)


def scatter_sum(n, x, near, far, staged, near_send, near_recv, far_send, far_recv):
    me, partner = places(n)
    half = n // 2

    def give(k):
        owner = lax.rem(partner + 2 * k, n)
        return remote(x.at[owner], near.at[k], near_send.at[k], near_recv.at[k], partner)

    def far_copy(k):
        return remote(staged.at[k], far.at[k], far_send.at[k], far_recv.at[k], lax.rem(me + 2 * k, n))

    def start(k, _):
        give(k).start()
        return 0

    lax.fori_loop(1, half, start, 0)
    give(0).start()

    def pair(k, _):
        give(k).wait_recv()
        staged[k] = x[lax.rem(me + 2 * k, n)] + near[k]
        far_copy(k).start()
        return 0

    lax.fori_loop(1, half, pair, 0)
    give(0).wait_recv()
    staged[0] = x[me] + near[0]

    def take(k, _):
        far_copy(k).wait_recv()
        staged[0] = staged[0] + far[k]
        return 0

    lax.fori_loop(1, half, take, 0)

    def sent(k, _):
        give(k).wait_send()
        return 0

    def far_sent(k, _):
        far_copy(k).wait_send()
        return 0

    lax.fori_loop(0, half, sent, 0)
    lax.fori_loop(1, half, far_sent, 0)
    return staged.at[0]


def gather_kernel(n, x, out, send, fwd, recv):
    greet(n)
    gather(n, x, out, send, fwd, recv)


def scatter_kernel(n, x, out, near, far, staged, *sems):
    greet(n)
    out[...] = scatter_sum(n, x, near, far, staged, *sems)[...]


def reduce_kernel(n, x, out, near, far, staged, near_send, near_recv, far_send, far_recv, send, fwd, recv):
    greet(n)
    own = scatter_sum(n, x, near, far, staged, near_send, near_recv, far_send, far_recv)
    gather(n, own, out, send, fwd, recv)


VM = pl.BlockSpec(memory_space=pltpu.VMEM)


def comm(body, n, name, ident, out_shape, scratch):
    return pl.pallas_call(
        functools.partial(body, n),
        out_shape=jax.ShapeDtypeStruct(out_shape, F32),
        in_specs=[VM],
        out_specs=VM,
        scratch_shapes=scratch,
        name=name,
        compiler_params=pltpu.CompilerParams(collective_id=ident, has_side_effects=True, vmem_limit_bytes=32 << 20),
    )


def sems(*counts):
    return [pltpu.SemaphoreType.DMA((c,)) for c in counts]


def pair_kernel(
    step,
    fam,
    cdd,
    masks,
    keep_rows,
    present_row,
    right,
    left,
    left_t,
    weights,
    right_terms,
    out_grad,
    left_grad,
    rt_hi,
    rt_lo,
    u_hi,
    u_lo,
    c_hi,
    c_lo,
):
    g = pl.program_id(0)
    width = left.shape[1]
    rows = left.shape[0] // fam
    pair = LANES

    @pl.when(g == 0)
    def _():
        hi, lo = split(right[...].T)
        rt_hi[...] = hi
        rt_lo[...] = lo
        l_hi, l_lo = split(left[...])
        l_three = jnp.concatenate([l_hi.astype(F32), l_hi.astype(F32), l_lo.astype(F32)], axis=1).astype(BF16)

        @pl.loop(0, width // 2)
        def _(q):
            lanes = pl.ds(pl.multiple_of(q * 2 * pair, 2 * pair), 2 * pair)
            w_hi, w_lo = split(weights[:, lanes])
            hi, lo = split(nn(l_three, jnp.concatenate([w_hi, w_lo, w_hi], axis=0)))
            for b in range(2):
                dest = pl.ds(pl.multiple_of((2 * q + b) * fam, fam), fam)
                for r in range(rows):
                    at = slice(r * pair, (r + 1) * pair)
                    u_hi[dest, at] = hi[r * fam : (r + 1) * fam, b * pair : (b + 1) * pair]
                    u_lo[dest, at] = lo[r * fam : (r + 1) * fam, b * pair : (b + 1) * pair]

        right_terms[...] = jnp.zeros_like(right_terms)

    count = nt(masks[...].astype(BF16), keep_rows[0].astype(BF16))
    factor = masks[:, fam : fam + 1] * present_row[0] / jnp.maximum(count, 1.0)
    s_hi, s_lo = split(jnp.concatenate([cdd[q] * factor[:, q : q + 1] for q in range(step)], axis=1))
    lanes = pl.ds(pl.multiple_of(g * step * pair, step * pair), step * pair)
    chunk_hi, chunk_lo = u_hi[:, lanes], u_lo[:, lanes]
    right_terms[...] += nt(s_hi, chunk_hi) + nt(s_hi, chunk_lo) + nt(s_lo, chunk_hi)
    hi, lo = split(nn(rt_hi[...], s_hi) + nn(rt_hi[...], s_lo) + nn(rt_lo[...], s_hi))
    c_hi[:, lanes] = hi
    c_lo[:, lanes] = lo

    @pl.when(g == pl.num_programs(0) - 1)
    def _():
        t_hi, t_lo = split(left_t[...])
        t_both = jnp.concatenate([t_hi, t_lo], axis=0)
        left_grad[...] = jnp.zeros_like(left_grad)

        @pl.loop(0, width // 2)
        def _(q):
            def regroup(ref):
                cols = []
                for c in range(2):
                    at = pl.ds(pl.multiple_of((2 * q + c) * fam, fam), fam)
                    cols.append(
                        jnp.concatenate([ref[at, r * pair : (r + 1) * pair] for r in range(rows)], axis=0)
                    )
                return jnp.concatenate(cols, axis=1)

            hi, lo = regroup(c_hi), regroup(c_lo)
            lanes = pl.ds(pl.multiple_of(q * 2 * pair, 2 * pair), 2 * pair)
            w_hi, w_lo = split(weights[:, lanes])
            left_grad[...] += nt(hi, w_hi) + nt(hi, w_lo) + nt(lo, w_hi)
            both = nn(t_both, hi)
            out_grad[:, lanes] = both[:width] + both[width:] + nn(t_hi, lo)


def pair_work(cdd, masks, keep_rows, present_row, right, left, left_t, weights, fam):
    rows, total, pair = cdd.shape
    width = left.shape[1]
    step = keep_rows.shape[1]
    feats = width * fam
    whole = lambda a: pl.BlockSpec(a.shape, lambda g: (0,) * a.ndim)
    return pl.pallas_call(
        functools.partial(pair_kernel, step, fam),
        grid=(rows // step,),
        out_shape=(
            jax.ShapeDtypeStruct((total, feats), F32),
            jax.ShapeDtypeStruct((width, width * pair), F32),
            jax.ShapeDtypeStruct((rows * fam, width), F32),
        ),
        in_specs=[
            pl.BlockSpec((step, total, pair), lambda g: (g, 0, 0)),
            whole(masks),
            pl.BlockSpec((1,) + keep_rows.shape[1:], lambda g: (g, 0, 0)),
            pl.BlockSpec((1,) + present_row.shape[1:], lambda g: (g, 0, 0)),
            whole(right),
            whole(left),
            whole(left_t),
            whole(weights),
        ],
        out_specs=(
            pl.BlockSpec((total, feats), lambda g: (0, 0)),
            pl.BlockSpec((width, width * pair), lambda g: (0, 0)),
            pl.BlockSpec((rows * fam, width), lambda g: (0, 0)),
        ),
        scratch_shapes=[pltpu.VMEM((feats, total), BF16)] * 2 + [pltpu.VMEM((feats, rows * pair), BF16)] * 4,
        name="pair_work",
        compiler_params=pltpu.CompilerParams(vmem_limit_bytes=60 << 20, dimension_semantics=("arbitrary",)),
    )(cdd, masks, keep_rows, present_row, right, left, left_t, weights)


def local(n, act, valid, flags, w_left, w_right, w_final, cdd):
    rows, total, pair = cdd.shape
    fam, _, depth = act.shape
    width = w_left.shape[1]
    feats = width * fam
    half = n // 2
    keep = valid.astype(F32)
    present = flags.astype(F32)
    left = jnp.einsum("srm,ma->rsa", act, w_left, precision=EXACT) * keep.T[:, :, None]
    right = jnp.einsum("srm,mc->rcs", act, w_right, precision=EXACT) * keep.T[:, None, :]
    marks = jnp.concatenate([keep.T, present[:, None], jnp.zeros((rows, LANES - fam - 1), F32)], axis=1)
    block = jnp.concatenate([right.reshape(rows, feats), marks], axis=1)
    everyone = comm(gather_kernel, n, "gather_right", 0, (n, rows, feats + LANES), sems(half, half, n))(block)
    everyone = everyone.reshape(total, feats + LANES)

    step = min(4, rows)
    keep_rows = jnp.concatenate([keep.T, jnp.zeros((rows, LANES - fam), F32)], axis=1).reshape(-1, step, LANES)
    flat = left.reshape(rows * fam, width)
    right_terms, out_grad, left_grad = pair_work(
        cdd,
        everyone[:, feats:],
        keep_rows,
        present.reshape(-1, 1, step),
        everyone[:, :feats],
        flat,
        flat.T,
        w_final.reshape(width, width * pair),
        fam,
    )
    slab = pltpu.VMEM((half, rows, feats), F32)
    mine = comm(
        scatter_kernel, n, "scatter_right", 1, (rows, feats), [slab] * 3 + sems(half, half, half, half)
    )(right_terms.reshape(n, rows, feats))

    left_grad = left_grad.reshape(rows, fam, width) * keep.T[:, :, None]
    right_grad = mine.reshape(rows, width, fam) * keep.T[:, None, :]
    both = jnp.concatenate([left_grad.transpose(1, 0, 2), right_grad.transpose(2, 0, 1)], axis=2)
    w_both = jnp.concatenate([w_left, w_right], axis=1)
    alignment = jnp.einsum("srz,mz->srm", both, w_both, precision=EXACT)
    grads = jnp.einsum("srm,srz->mz", act, both, precision=EXACT)

    tail = 2 * depth * width // LANES
    used = width * width + tail
    piece = -(-used // (8 * n)) * 8
    packed = jnp.concatenate(
        [out_grad.reshape(width * width, pair), grads.reshape(tail, LANES), jnp.zeros((piece * n - used, LANES), F32)]
    )
    slab = pltpu.VMEM((half, piece, LANES), F32)
    summed = comm(
        reduce_kernel,
        n,
        "reduce_weights",
        2,
        (n, piece, LANES),
        [slab] * 3 + sems(half, half, half, half, half, half, n),
    )(packed.reshape(n, piece, LANES)).reshape(n * piece, LANES)
    grads = summed[width * width : used].reshape(depth, 2 * width)
    return alignment, grads[:, :width], grads[:, width:], summed[: width * width]


def solution(mesh):
    in_specs = (
        P("groups", "row", None),
        P("groups", "row"),
        P(("groups", "row")),
        P(),
        P(),
        P(),
        P(("groups", "row"), None, None),
    )
    out_specs = (P("groups", "row", None), P("groups", None), P("groups", None), P("groups", None))
    body = functools.partial(local, mesh.shape["row"])
    return jax.shard_map(body, mesh=mesh, in_specs=in_specs, out_specs=out_specs, check_vma=False)
```

time: 461 us -> 114 us (0.25); the launches traced: 453 us -> 113 us
  waiting for transfers between devices: 183 us -> 0 us
  matrix products: 170 us -> 6.51 us
  Pallas kernels: 0 us -> 91.3 us
  blocking collectives: 53.4 us -> 0 us
  between operations: 14.8 us -> 0.81 us
  other arithmetic: 11.2 us -> 1.65 us
  local copies, waits for them, and re-layouts: 19.9 us -> 12.6 us
    psum x2 -> x0, waiting for transfers between devices: 183 us -> none  [the longest x1 97.9 us: local(): summed = lax.psum(right_terms, 'row')]
    dot_general x14 -> x4, matrix products: 170 us -> 6.51 us  [the longest x1 2.06 us: local(): jnp.einsum('srm,ma->rsa', act, w_left, precision=EXACT) * keep.T[:, :, None]]
    pallas_call x0 -> x4, Pallas kernels: none -> 91.3 us  [the longest x1 31.9 us: pair_work(): pl.pallas_call(functools.partial(pair_kernel, step, fam), grid=(rows // s...]
    unnamed x1 -> x0, blocking collectives: 29.9 us -> none
    all_gather x1 -> x0, blocking collectives: 23.5 us -> none  [local(): lax.all_gather(keep_mask, 'row', axis=0, tiled=True)]
    unnamed x19 -> x12, local copies, waits for them, and re-layouts: 10.3 us -> 2.62 us
    dot_general x3 -> x1, local copies, waits for them, and re-layouts: 7.12 us -> 0.09 us  [local(): grads = jnp.einsum('srm,srz->mz', act, both, precision=EXACT)]
    mul x1 -> x0, other arithmetic: 5.26 us -> none  [local(): scaled = couple_delta_deriv * factor[:, :, None]]
  transfers between devices with their start and end apart: 3 -> 0, of which waited for: 2 -> 0; matrix products, arithmetic and copies ran while one was open for 35% -> 0% of each run, Pallas kernels for 0% -> 0%
where the time goes in v1:
time: 114 us; the launch traced here: 113 us
  Pallas kernels  91.3 us (80%)
  local copies, waits for them, and re-layouts  12.6 us (11%)
  matrix products  6.51 us (6%)
  other arithmetic  1.65 us (1%)
    pallas_call x1, Pallas kernels, pair_work(): pl.pallas_call(functools.partial(pair_kernel, step, fam), grid=(rows // s...  31.9 us
    pallas_call x1, Pallas kernels, local(): comm(reduce_kernel, n, 'reduce_weights', 2, (n, piece, LANES), [slab] * 3...  23.2 us
    pallas_call x1, Pallas kernels, local(): comm(scatter_kernel, n, 'scatter_right', 1, (rows, feats), [slab] * 3 + s...  18.2 us
    pallas_call x1, Pallas kernels, local(): comm(gather_kernel, n, 'gather_right', 0, (n, rows, feats + LANES), sems(...  18 us
    unnamed x12, local copies, waits for them, and re-layouts  2.62 us

profile of v1, /device:TPU:0, one launch (start us, length us, event | category | flops | bytes accessed | tf_op | source)
XLA Modules:
  0.0 112.9 jit_solution(1882072228900836048)
XLA Ops:
  0.6 0.7 fusion.11
  1.4 0.7 reshape.55
  2.2 0.7 convert_bitcast_fusion.1
  3.0 0.6 concatenate.16
  3.6 2.1 %fusion.1 = f32[32,32,16]{0,1,2:T(8,128)S(1)} fusion(f32[16,32,256]{2,1,0:T(8,128)S(1)} %copy-done, f32[32,16]{0,1:T(8,128)S(1)} %get-tuple-element.20, f32[256,32]{0,1:T(8,128)} %param.11), kind=kOutput, calls=%fused_computation.3 | convolution fusion | flops 50348032 | bytes 624640 | tf_op jit(solution)/shard_map/srm,mc->rcs/dot_general | solution.py:306
  5.7 0.2 copy.44
  6.0 2.1 %fusion = f32[32,16,32]{0,2,1:T(8,128)S(1)} fusion(f32[16,32,256]{2,1,0:T(8,128)S(1)} %copy-done, f32[32,16]{0,1:T(8,128)S(1)} %get-tuple-element.20, f32[256,32]{0,1:T(8,128)} %param.10), kind=kOutput, calls=%fused_computation.1 | convolution fusion | flops 50348032 | bytes 624640 | tf_op jit(solution)/shard_map/srm,ma->rsa/dot_general | solution.py:305
  8.1 0.2 copy.48
  8.3 0.7 copy.49
  9.0 1.9 %reshape.57.weights = f32[32,4096]{1,0:T(8,128)} reshape(f32[1024,128]{1,0:T(8,128)} %param.12) | data formatting | bytes 1048576 | tf_op jit(solution)/shard_map/reshape | solution.py:323
  10.9 18.0 %gather_right.1 = f32[16,32,640]{2,1,0:T(8,128)S(1)} custom-call(f32[32,640]{1,0:T(8,128)S(1)} %maximum_maximum_fusion.x), custom_call_target="tpu_custom_call" | custom-call | tf_op jit(solution)/shard_map/gather_right/pallas_call | solution.py:309
  28.9 0.7 slice.24.masks
  29.6 1.1 slice.25.right
  30.7 31.9 %pair_work.1 = (f32[512,512]{1,0:T(8,128)}, f32[32,4096]{1,0:T(8,128)}, f32[512,32]{1,0:T(8,128)}) custom-call(f32[32,512,128]{2,1,0:T(8,128)} %cdd.1, f32[512,128]{1,0:T(8,128)} %slice.24.masks, f32[8,4,128]{2,1,0:T(4,128)} %bitcast.59, f32[8,1,4]{2,1,0:T(1,128)} %bitcast.60, f32[512,512]{1,0:T(8,128)} %slice.25.right, f32[512,32]{1,0:T(8,128)} %bitcast.52, ...), custom_call_target="tpu_custom_call" | custom-call | tf_op jit(solution)/shard_map/pair_work/pallas_call | solution.py:268
  62.6 1.1 copy.51
  63.8 1.2 %copy-done.1 = f32[512,512]{1,0:T(8,128)S(1)} copy-done((f32[512,512]{1,0:T(8,128)S(1)}, f32[512,512]{1,0:T(8,128)}, u32[]{:S(2)}) %copy-start.1) | copy-done | bytes 1048600
  65.0 18.2 %scatter_right.1 = f32[32,512]{1,0:T(8,128)S(1)} custom-call(f32[16,32,512]{2,1,0:T(8,128)S(1)} %bitcast.50), custom_call_target="tpu_custom_call" | custom-call | tf_op jit(solution)/shard_map/scatter_right/pallas_call | solution.py:327
  83.5 0.6 convolution_bitcast_fusion.2
  84.1 1.8 %fusion.2 = f32[16,32,256]{2,1,0:T(8,128)} fusion(f32[16,32,32]{1,2,0:T(8,128)S(1)} %fusion.3, f32[16,32,32]{1,2,0:T(8,128)S(1)} %multiply_bitcast_fusion, f32[256,32]{0,1:T(8,128)S(1)} %copy-done.3, f32[256,32]{0,1:T(8,128)S(1)} %copy-done.4), kind=kOutput, calls=%fused_computation.7 | convolution fusion | flops 100712448 | bytes 720896 | tf_op jit(solution)/shard_map/srz,mz->srm/dot_general | solution.py:335
  86.1 1.1 reshape.61
  87.3 23.2 %reduce_weights.1 = f32[16,72,128]{2,1,0:T(8,128)S(1)} custom-call(f32[16,72,128]{2,1,0:T(8,128)S(1)} %bitcast.47), custom_call_target="tpu_custom_call" | custom-call | tf_op jit(solution)/shard_map/reduce_weights/pallas_call | solution.py:345
  110.5 0.8 slice.29
  111.5 0.7 copy.58
  112.2 0.7 copy.57
  (24 shorter events, 1.1 us)
Async XLA Ops:
  0.6 3.0 %copy-start = (f32[16,32,256]{2,1,0:T(8,128)S(1)}, f32[16,32,256]{2,1,0:T(8,128)}, u32[]{:S(2)}) copy-start(f32[16,32,256]{2,1,0:T(8,128)} %param.7) | copy-start | bytes 1572868
  8.2 22.5 %copy-start.2 = (f32[32,16,32]{2,1,0:T(8,128)}, f32[32,16,32]{2,1,0:T(8,128)S(1)}, u32[]{:S(2)}) copy-start(f32[32,16,32]{2,1,0:T(8,128)S(1)} %copy.48) | copy-start | bytes 196612
  29.6 54.5 %copy-start.3 = (f32[256,32]{0,1:T(8,128)S(1)}, f32[256,32]{0,1:T(8,128)}, u32[]{:S(2)}) copy-start(f32[256,32]{0,1:T(8,128)} %param.11) | copy-start | bytes 98308
  29.6 54.5 %copy-start.4 = (f32[256,32]{0,1:T(8,128)S(1)}, f32[256,32]{0,1:T(8,128)}, u32[]{:S(2)}) copy-start(f32[256,32]{0,1:T(8,128)} %param.10) | copy-start | bytes 98308
  63.8 1.2 %copy-start.1 = (f32[512,512]{1,0:T(8,128)S(1)}, f32[512,512]{1,0:T(8,128)}, u32[]{:S(2)}) copy-start(f32[512,512]{1,0:T(8,128)} %get-tuple-element.8) | copy-start | bytes 3145732

commit v2 on v0

v2 whole, which is shorter than its diff:
```python
import functools

import jax
import jax.numpy as jnp
from jax import lax
from jax.experimental import pallas as pl
from jax.experimental.pallas import tpu as pltpu
from jax.sharding import PartitionSpec as P

F32, BF16 = jnp.float32, jnp.bfloat16
LANES = 128


def split(x):
    hi = x.astype(BF16)
    return hi, (x - hi.astype(F32)).astype(BF16)


def nn(a, b):
    return jnp.dot(a, b, preferred_element_type=F32)


def nt(a, b):
    return lax.dot_general(a, b, (((1,), (1,)), ((), ())), preferred_element_type=F32)


def remote(src, dst, send, recv, target):
    return pltpu.make_async_remote_copy(
        src_ref=src,
        dst_ref=dst,
        send_sem=send,
        recv_sem=recv,
        device_id={"row": target},
        device_id_type=pl.DeviceIdType.MESH,
    )


def each(start, stop, body):
    def one(k, _):
        body(k)
        return 0

    lax.fori_loop(start, stop, one, 0)


def sides(n):
    half, across = n // 2, 1
    while half % (2 * across) == 0 and 4 * across * across <= half:
        across *= 2
    return half // across, across


class Place:
    def __init__(self, n):
        self.n = n
        self.deep, self.wide = sides(n)
        self.me = lax.axis_index("row")
        self.core = lax.rem(self.me, 2)
        chip = lax.div(self.me, 2)
        self.x = lax.rem(chip, self.wide)
        self.z = lax.div(chip, self.wide)
        self.partner = self.at(0, 0, True)

    def at(self, k, m, other=False):
        z = lax.rem(self.z + k + self.deep, self.deep)
        x = lax.rem(self.x + m + self.wide, self.wide)
        core = 1 - self.core if other else self.core
        return (z * self.wide + x) * 2 + core

    def signal(self):
        barrier = pltpu.get_barrier_semaphore()

        def tell(target):
            pl.semaphore_signal(barrier, inc=1, device_id={"row": target}, device_id_type=pl.DeviceIdType.MESH)

        tell(self.partner)
        each(1, self.wide, lambda m: tell(self.at(0, m)))
        each(1, self.deep, lambda k: tell(self.at(k, 0)))

    def wait(self):
        pl.semaphore_wait(pltpu.get_barrier_semaphore(), self.deep + self.wide - 1)


class Gather:
    def __init__(self, place, own, out, z_send, x_send, c_send, recv):
        self.p, self.own, self.out = place, own, out
        self.z_send, self.x_send, self.c_send, self.recv = z_send, x_send, c_send, recv

    def copy(self, src, owner, send, target):
        return remote(src, self.out(owner), send, self.recv.at[owner], target)

    def start(self):
        p = self.p
        each(1, p.deep, lambda k: self.copy(self.own, p.me, self.z_send.at[k], p.at(k, 0)).start())
        each(1, p.wide, lambda m: self.copy(self.own, p.me, self.x_send.at[m], p.at(0, m)).start())
        self.copy(self.own, p.me, self.c_send.at[0], p.partner).start()

    def landed(self, owner):
        self.copy(self.out(owner), owner, self.z_send.at[0], self.p.partner).wait_recv()

    def cross(self):
        p = self.p

        def one(k):
            owner = p.at(-k, 0)
            self.landed(owner)
            block = self.out(owner)
            each(1, p.wide, lambda m: self.copy(block, owner, self.x_send.at[k * p.wide + m], p.at(0, m)).start())
            self.copy(block, owner, self.c_send.at[k * p.wide], p.partner).start()

        each(1, p.deep, one)

    def pair(self):
        p = self.p

        def one(k):
            def two(m):
                owner = p.at(-k, -m)
                self.landed(owner)
                self.copy(self.out(owner), owner, self.c_send.at[k * p.wide + m], p.partner).start()

            each(1, p.wide, two)

        each(0, p.deep, one)

    def finish(self):
        p = self.p
        each(0, p.deep, lambda k: each(0, p.wide, lambda m: self.landed(p.at(-k, -m, True))))

        def sent(sem):
            self.copy(self.own, p.me, sem, p.partner).wait_send()

        each(1, p.deep, lambda k: sent(self.z_send.at[k]))
        each(0, p.deep, lambda k: each(1, p.wide, lambda m: sent(self.x_send.at[k * p.wide + m])))
        each(0, p.deep * p.wide, lambda i: sent(self.c_send.at[i]))


class Scatter:
    def __init__(self, place, x, near, mid, far, staged, *sems):
        self.p, self.x, self.near, self.mid, self.far, self.staged = place, x, near, mid, far, staged
        self.near_send, self.near_recv, self.mid_send, self.mid_recv, self.far_send, self.far_recv = sems

    def near_copy(self, k, m):
        p, i = self.p, k * self.p.wide + m
        return remote(
            self.x(p.at(k, m, True)), self.near.at[i], self.near_send.at[i], self.near_recv.at[i], p.partner
        )

    def mid_copy(self, k, m):
        p, i = self.p, k * self.p.wide + m
        return remote(self.staged.at[i], self.mid.at[i], self.mid_send.at[i], self.mid_recv.at[i], p.at(0, m))

    def far_copy(self, k):
        p = self.p
        return remote(
            self.staged.at[k * p.wide], self.far.at[k], self.far_send.at[k], self.far_recv.at[k], p.at(k, 0)
        )

    def over(self, first, body):
        p = self.p
        each(0, p.deep, lambda k: each(first, p.wide, lambda m: body(k, m)))

    def start(self):
        self.over(1, lambda k, m: self.near_copy(k, m).start())
        each(0, self.p.deep, lambda k: self.near_copy(k, 0).start())

    def pair(self):
        p = self.p

        def merge(k, m):
            i = k * p.wide + m
            self.near_copy(k, m).wait_recv()
            self.staged[i] = self.x(p.at(k, m))[...] + self.near[i]

        def pass_on(k, m):
            merge(k, m)
            self.mid_copy(k, m).start()

        self.over(1, pass_on)
        each(0, p.deep, lambda k: merge(k, 0))

    def cross(self):
        p = self.p

        def merge(k):
            i = k * p.wide

            def one(m):
                self.mid_copy(k, m).wait_recv()
                self.staged[i] = self.staged[i] + self.mid[i + m]

            each(1, p.wide, one)

        def pass_on(k):
            merge(k)
            self.far_copy(k).start()

        each(1, p.deep, pass_on)
        merge(0)

    def finish(self):
        def one(k):
            self.far_copy(k).wait_recv()
            self.staged[0] = self.staged[0] + self.far[k]

        each(1, self.p.deep, one)
        self.over(0, lambda k, m: self.near_copy(k, m).wait_send())
        self.over(1, lambda k, m: self.mid_copy(k, m).wait_send())
        each(1, self.p.deep, lambda k: self.far_copy(k).wait_send())


def gather_sems(n):
    deep, wide = sides(n)
    return [pltpu.SemaphoreType.DMA((c,)) for c in (deep, deep * wide, deep * wide, n)]


def scatter_scratch(n, block):
    deep, wide = sides(n)
    most = deep * wide
    return [pltpu.VMEM((c,) + block, F32) for c in (most, most, deep, most)] + [
        pltpu.SemaphoreType.DMA((c,)) for c in (most, most, most, most, deep, deep)
    ]


def three(dot, a, b):
    a_hi, a_lo = split(a)
    b_hi, b_lo = split(b)
    return dot(a_hi, b_hi) + dot(a_hi, b_lo) + dot(a_lo, b_hi)


def kernel(
    n,
    step,
    fam,
    act,
    keep_t,
    marks,
    keep_rows,
    present_row,
    w_cat,
    w_final,
    cdd_hbm,
    align,
    left_w,
    right_w,
    out_w,
    *scratch,
):
    scratch = list(scratch)

    def take(count):
        taken = scratch[:count]
        del scratch[:count]
        return taken

    cdd, u, s_hi, s_lo, c_hi, c_lo, terms, terms_split = take(8)
    left, own_right, marks_all, right_all, flat_marks, turned, rt_hi, rt_lo, left_grad, both, packed, total_sum = take(12)
    (load,) = take(1)
    mark_sems, right_sems, sum_sems = take(4), take(4), take(4)
    right_scatter, sum_scatter = take(10), take(10)
    assert not scratch

    rows, total, pair = cdd.shape
    width = w_cat.shape[1] // 2
    groups = rows // step
    piece = packed.shape[0] // n
    place = Place(n)
    place.signal()

    def fetch(g):
        at = pl.ds(g * step, step)
        return pltpu.make_async_copy(cdd_hbm.at[at], cdd.at[at], load.at[g])

    each(0, groups, lambda g: fetch(g).start())

    projected = three(nn, act[...], w_cat[...])
    rights = []
    for s in range(fam):
        one = projected[s * rows : (s + 1) * rows] * keep_t[:, s : s + 1]
        rights.append(one[:, width:])
        left[pl.ds(s, rows, stride=fam), :] = jnp.concatenate([one, jnp.zeros((rows, LANES - 2 * width), F32)], axis=1)
    own_right[...] = jnp.concatenate(rights, axis=1)

    mark_gather = Gather(place, marks, lambda o: marks_all.at[o], *mark_sems)
    right_gather = Gather(place, own_right, lambda o: right_all.at[o], *right_sems)
    place.wait()
    mark_gather.start()
    right_gather.start()
    marks_all[place.me] = marks[...]
    right_all[place.me] = own_right[...]

    def weights(q):
        parts = [w_final[pl.ds(2 * q + b, width, stride=width), :] for b in range(2)]
        return jnp.concatenate(parts, axis=1)

    l_hi, l_lo = split(left[:, :width])
    l_three = jnp.concatenate([l_hi.astype(F32), l_hi.astype(F32), l_lo.astype(F32)], axis=1).astype(BF16)

    def make_u(q):
        w_hi, w_lo = split(weights(q))
        value = nn(l_three, jnp.concatenate([w_hi, w_lo, w_hi], axis=0))
        for b in range(2):
            for r in range(rows):
                u[r, pl.ds(2 * q + b, fam, stride=width), :] = value[
                    r * fam : (r + 1) * fam, b * pair : (b + 1) * pair
                ]

    each(0, width // 4, make_u)
    mark_gather.cross()
    each(width // 4, width // 2, make_u)
    mark_gather.pair()
    right_gather.cross()
    terms[...] = jnp.zeros_like(terms)
    mark_gather.finish()
    for o in range(n):
        flat_marks[o * rows : (o + 1) * rows, :] = marks_all[o]

    def lanes_of(g):
        return pl.ds(pl.multiple_of(g * step * pair, step * pair), step * pair)

    def make_terms(g):
        fetch(g).wait()
        count = nt(flat_marks[...].astype(BF16), keep_rows[g].astype(BF16))
        factor = flat_marks[:, fam : fam + 1] * present_row[g] / jnp.maximum(count, 1.0)
        hi, lo = split(jnp.concatenate([cdd[g * step + q] * factor[:, q : q + 1] for q in range(step)], axis=1))
        lanes = lanes_of(g)
        s_hi[:, lanes] = hi
        s_lo[:, lanes] = lo
        u_hi, u_lo = split(jnp.concatenate([u[g * step + q] for q in range(step)], axis=1))
        terms[...] += nt(hi, u_hi) + nt(hi, u_lo) + nt(lo, u_hi)

    each(0, groups // 4, make_terms)
    right_gather.pair()
    each(groups // 4, groups, make_terms)
    right_gather.finish()

    for o in range(n):
        terms_split[o] = terms[o * rows : (o + 1) * rows, :]
    right_sum = Scatter(place, lambda o: terms_split.at[o], *right_scatter)
    right_sum.start()
    for o in range(n):
        terms[o * rows : (o + 1) * rows, :] = right_all[o]
    for t in range(total // LANES):
        at = slice(t * LANES, (t + 1) * LANES)
        turned[t] = terms[at, :].T
        for c in range(width):
            hi, lo = split(turned[t, pl.ds(c, fam, stride=width), :])
            rt_hi[c * fam : (c + 1) * fam, at] = hi
            rt_lo[c * fam : (c + 1) * fam, at] = lo

    def make_carried(g):
        lanes = lanes_of(g)
        hi, lo = split(
            nn(rt_hi[...], s_hi[:, lanes]) + nn(rt_hi[...], s_lo[:, lanes]) + nn(rt_lo[...], s_hi[:, lanes])
        )
        c_hi[:, lanes] = hi
        c_lo[:, lanes] = lo

    each(0, groups // 4, make_carried)
    right_sum.pair()
    each(groups // 4, 3 * groups // 4, make_carried)
    right_sum.cross()
    each(3 * groups // 4, groups, make_carried)

    t_hi, t_lo = split(left[...].T[:width])
    t_both = jnp.concatenate([t_hi, t_lo], axis=0)
    left_grad[...] = jnp.zeros_like(left_grad)

    def contract(q):
        def regroup(ref):
            cols = []
            for c in range(2):
                at = pl.ds(pl.multiple_of((2 * q + c) * fam, fam), fam)
                cols.append(jnp.concatenate([ref[at, r * pair : (r + 1) * pair] for r in range(rows)], axis=0))
            return jnp.concatenate(cols, axis=1)

        hi, lo = regroup(c_hi), regroup(c_lo)
        w_hi, w_lo = split(weights(q))
        left_grad[:, :width] += nt(hi, w_hi) + nt(hi, w_lo) + nt(lo, w_hi)
        two = nn(t_both, hi)
        value = two[:width] + two[width:] + nn(t_hi, lo)
        for c in range(2):
            at = pl.ds(pl.multiple_of((2 * q + c) * width, width), width)
            packed[at, :] = value[:, c * pair : (c + 1) * pair]

    each(0, width // 2, contract)
    right_sum.finish()

    mine = right_scatter[3]
    for s in range(fam):
        one = jnp.concatenate(
            [left_grad[pl.ds(s, rows, stride=fam), :][:, :width], mine[0, :, s * width : (s + 1) * width]], axis=1
        )
        both[s * rows : (s + 1) * rows, :] = jnp.concatenate(
            [one * keep_t[:, s : s + 1], jnp.zeros((rows, LANES - 2 * width), F32)], axis=1
        )
    grads = three(nn, both[...].T, act[...])[: 2 * width]
    base = width * width
    tiles = act.shape[1] // LANES
    for t in range(tiles):
        packed[base + t * 2 * width : base + (t + 1) * 2 * width, :] = grads[:, t * LANES : (t + 1) * LANES]
    end = base + tiles * 2 * width
    if end < packed.shape[0]:
        packed[end:, :] = jnp.zeros((packed.shape[0] - end, LANES), F32)

    def piece_of(ref):
        return lambda o: ref.at[pl.ds(pl.multiple_of(o * piece, 8), piece), :]

    weight_sum = Scatter(place, piece_of(packed), *sum_scatter)
    weight_sum.start()
    align[...] = three(nt, both[:, : 2 * width], w_cat[...])
    weight_sum.pair()
    weight_sum.cross()
    weight_sum.finish()
    summed = sum_scatter[3]
    spread = Gather(place, summed.at[0], piece_of(total_sum), *sum_sems)
    spread.start()
    total_sum[pl.ds(pl.multiple_of(place.me * piece, 8), piece), :] = summed[0]
    spread.cross()
    spread.pair()
    spread.finish()

    for c in range(width):
        out_w[pl.ds(c, width, stride=width), :] = total_sum[c * width : (c + 1) * width, :]
    for t in range(tiles):
        at = slice(t * LANES, (t + 1) * LANES)
        part = total_sum[base + t * 2 * width : base + (t + 1) * 2 * width, :]
        part = jnp.concatenate([part, jnp.zeros((LANES - 2 * width, LANES), F32)], axis=0).T
        left_w[at, :] = part[:, :width]
        right_w[at, :] = part[:, width : 2 * width]


def local(n, act, valid, flags, w_left, w_right, w_final, cdd):
    rows, total, pair = cdd.shape
    fam, _, depth = act.shape
    width = w_left.shape[1]
    feats = width * fam
    keep_t = valid.astype(F32).T
    present = flags.astype(F32)
    marks = jnp.concatenate([keep_t, present[:, None], jnp.zeros((rows, LANES - fam - 1), F32)], axis=1)
    step = min(4, rows)
    keep_rows = jnp.concatenate([keep_t, jnp.zeros((rows, LANES - fam), F32)], axis=1).reshape(-1, step, LANES)
    used = width * width + 2 * depth * width // LANES
    piece = -(-used // (8 * n)) * 8
    vm = pl.BlockSpec(memory_space=pltpu.VMEM)
    f32 = lambda *shape: pltpu.VMEM(shape, F32)
    b16 = lambda *shape: pltpu.VMEM(shape, BF16)
    align, left_w, right_w, out_w = pl.pallas_call(
        functools.partial(kernel, n, step, fam),
        out_shape=tuple(
            jax.ShapeDtypeStruct(shape, F32)
            for shape in ((fam * rows, depth), (depth, width), (depth, width), (width * width, pair))
        ),
        in_specs=[vm] * 7 + [pl.BlockSpec(memory_space=pl.ANY)],
        out_specs=(vm,) * 4,
        scratch_shapes=[
            f32(rows, total, pair),
            f32(rows, feats, pair),
            b16(total, rows * pair),
            b16(total, rows * pair),
            b16(feats, rows * pair),
            b16(feats, rows * pair),
            f32(total, feats),
            f32(n, rows, feats),
            f32(rows * fam, LANES),
            f32(rows, feats),
            f32(n, rows, LANES),
            f32(n, rows, feats),
            f32(total, LANES),
            f32(total // LANES, feats, LANES),
            b16(feats, total),
            b16(feats, total),
            f32(rows * fam, LANES),
            f32(fam * rows, LANES),
            f32(n * piece, LANES),
            f32(n * piece, LANES),
            pltpu.SemaphoreType.DMA((rows // step,)),
        ]
        + gather_sems(n) * 3
        + scatter_scratch(n, (rows, feats))
        + scatter_scratch(n, (piece, LANES)),
        name="outer_mean_grad",
        compiler_params=pltpu.CompilerParams(collective_id=0, has_side_effects=True, vmem_limit_bytes=60 << 20),
    )(
        act.reshape(fam * rows, depth),
        keep_t,
        marks,
        keep_rows,
        present.reshape(-1, 1, step),
        jnp.concatenate([w_left, w_right], axis=1),
        w_final,
        cdd,
    )
    return align.reshape(fam, rows, depth), left_w, right_w, out_w


def solution(mesh):
    in_specs = (
        P("groups", "row", None),
        P("groups", "row"),
        P(("groups", "row")),
        P(),
        P(),
        P(),
        P(("groups", "row"), None, None),
    )
    out_specs = (P("groups", "row", None), P("groups", None), P("groups", None), P("groups", None))
    body = functools.partial(local, mesh.shape["row"])
    return jax.shard_map(body, mesh=mesh, in_specs=in_specs, out_specs=out_specs, check_vma=False)
```

time: 461 us -> 84.8 us (0.18); the launches traced: 453 us -> 84.3 us
  waiting for transfers between devices: 183 us -> 0 us
  matrix products: 170 us -> 0 us
  Pallas kernels: 0 us -> 71.3 us
  blocking collectives: 53.4 us -> 0 us
  between operations: 14.8 us -> 0.65 us
  local copies, waits for them, and re-layouts: 19.9 us -> 9.56 us
  other arithmetic: 11.2 us -> 2.8 us
    psum x2 -> x0, waiting for transfers between devices: 183 us -> none  [the longest x1 97.9 us: local(): summed = lax.psum(right_terms, 'row')]
    dot_general x14 -> x0, matrix products: 170 us -> none  [the longest x2 61.7 us: local(): feats = jnp.einsum('rjk,abk->rjab', piece, w_three, precision=SPLIT_PIECES)]
    pallas_call x0 -> x1, Pallas kernels: none -> 71.3 us  [local(): pl.pallas_call(functools.partial(kernel, n, step, fam), out_shape=tuple((...]
    unnamed x1 -> x0, blocking collectives: 29.9 us -> none
    all_gather x1 -> x0, blocking collectives: 23.5 us -> none  [local(): lax.all_gather(keep_mask, 'row', axis=0, tiled=True)]
    dot_general x3 -> x0, local copies, waits for them, and re-layouts: 7.12 us -> none  [the longest x2 6.01 us: local(): jnp.einsum('rjab,rsa->jsb', feats, first_factor_embed, precision=SPLIT_PI...]
    mul x1 -> x0, other arithmetic: 5.26 us -> none  [local(): scaled = couple_delta_deriv * factor[:, :, None]]
    unnamed x19 -> x8, local copies, waits for them, and re-layouts: 10.3 us -> 8.65 us
  transfers between devices with their start and end apart: 3 -> 0, of which waited for: 2 -> 0; matrix products, arithmetic and copies ran while one was open for 35% -> 0% of each run, Pallas kernels for 0% -> 0%
where the time goes in v2:
time: 84.8 us; the launch traced here: 84.3 us
  Pallas kernels  71.3 us (84%)
  local copies, waits for them, and re-layouts  9.56 us (11%)
  other arithmetic  2.8 us (3%)
    pallas_call x1, Pallas kernels, local(): pl.pallas_call(functools.partial(kernel, n, step, fam), out_shape=tuple((...  71.3 us
    unnamed x8, local copies, waits for them, and re-layouts  8.65 us

profile of v2, /device:TPU:0, one launch (start us, length us, event | category | flops | bytes accessed | tf_op | source)
XLA Modules:
  0.0 84.3 jit_solution(15691367509541786749)
XLA Ops:
  0.6 0.1 pad.5.clone
  0.7 0.7 fusion.1
  1.4 0.7 reshape.22
  2.0 0.7 convert_element_type.6
  2.7 0.1 copy.25
  2.8 0.0 copy-start
  2.8 0.1 copy.26
  2.9 0.7 fusion
  3.6 0.9 %copy.27 = f32[256,32]{1,0:T(8,128)S(1)} copy(f32[256,32]{0,1:T(8,128)} %param.10) | data formatting | bytes 65536 | tf_op args[3]
  4.4 0.9 %copy.28 = f32[256,32]{1,0:T(8,128)S(1)} copy(f32[256,32]{0,1:T(8,128)} %param.11) | data formatting | bytes 65536 | tf_op args[4]
  5.3 0.8 pad_maximum_fusion.w_cat
  6.1 0.0 copy-done
  6.1 71.3 %outer_mean_grad.1 = (f32[512,256]{1,0:T(8,128)}, f32[256,32]{1,0:T(8,128)}, f32[256,32]{1,0:T(8,128)}, f32[1024,128]{1,0:T(8,128)}) custom-call(f32[512,256]{1,0:T(8,128)} %bitcast.7, f32[32,16]{1,0:T(8,128)} %bitcast.10, f32[32,128]{1,0:T(8,128)} %get-tuple-element.25.marks, f32[8,4,128]{2,1,0:T(4,128)} %bitcast.11, f32[8,1,4]{2,1,0:T(1,128)} %bitcast.12, ...), custom_call_target="tpu_custom_call" | custom-call | tf_op jit(solution)/shard_map/outer_mean_grad/pallas_call | solution.py:448
  77.4 1.6 %copy.30 = f32[256,32]{0,1:T(8,128)} copy(f32[256,32]{1,0:T(8,128)} %get-tuple-element.21) | data formatting | bytes 65536
  79.0 1.6 %copy.31 = f32[256,32]{0,1:T(8,128)} copy(f32[256,32]{1,0:T(8,128)} %get-tuple-element.22) | data formatting | bytes 65536
  80.5 1.9 %copy.34 = f32[16,32,256]{2,1,0:T(8,128)} copy(f32[16,32,256]{2,1,0:T(8,128)} %bitcast.8) | data formatting | bytes 1048576
  82.4 1.9 %copy.35 = f32[1024,128]{1,0:T(8,128)} copy(f32[1024,128]{1,0:T(8,128)} %get-tuple-element.35) | data formatting | bytes 1048576
  (1 shorter events, 0.0 us)
Async XLA Ops:
  2.8 3.3 %copy-start = (f32[16,32]{0,1:T(8,128)}, f32[16,32]{0,1:T(8,128)S(1)}, u32[]{:S(2)}) copy-start(f32[16,32]{0,1:T(8,128)S(1)} %copy.25) | copy-start | bytes 6148

commit v3 on v2

--- a/solution.py
+++ b/solution.py
@@ -233,17 +233,14 @@
     step,
     fam,
     act,
-    keep_t,
-    marks,
-    keep_rows,
-    present_row,
-    w_cat,
+    valid,
+    flags,
+    w_left,
+    w_right,
     w_final,
     cdd_hbm,
     align,
-    left_w,
-    right_w,
-    out_w,
+    total_sum,
     *scratch,
 ):
     scratch = list(scratch)
@@ -254,14 +251,15 @@
         return taken
 
     cdd, u, s_hi, s_lo, c_hi, c_lo, terms, terms_split = take(8)
-    left, own_right, marks_all, right_all, flat_marks, turned, rt_hi, rt_lo, left_grad, both, packed, total_sum = take(12)
+    left, own_right, marks_all, right_all, flat_marks, turned, rt_hi, rt_lo, left_grad, both, packed = take(11)
+    board, marks, keep_rows, present_row = take(4)
     (load,) = take(1)
     mark_sems, right_sems, sum_sems = take(4), take(4), take(4)
     right_scatter, sum_scatter = take(10), take(10)
     assert not scratch
 
     rows, total, pair = cdd.shape
-    width = w_cat.shape[1] // 2
+    width = w_left.shape[0]
     groups = rows // step
     piece = packed.shape[0] // n
     place = Place(n)
@@ -273,7 +271,19 @@
 
     each(0, groups, lambda g: fetch(g).start())
 
-    projected = three(nn, act[...], w_cat[...])
+    board[...] = jnp.zeros_like(board)
+    board[:fam, :rows] = valid[...].astype(F32)
+    board[fam : fam + 1, :rows] = flags[...].astype(F32)
+    marks[...] = board[...].T[:rows]
+    keep_t = marks[:, :fam]
+    lane = lax.broadcasted_iota(jnp.int32, (rows, LANES), 1)
+    kept = jnp.where(lane < fam, marks[...], 0.0)
+    for g in range(groups):
+        keep_rows[g] = kept[g * step : (g + 1) * step]
+        present_row[g] = board[fam : fam + 1, g * step : (g + 1) * step]
+
+    w_cat = jnp.concatenate([w_left[...], w_right[...]], axis=0)
+    projected = three(nt, act[...], w_cat)
     rights = []
     for s in range(fam):
         one = projected[s * rows : (s + 1) * rows] * keep_t[:, s : s + 1]
@@ -408,7 +418,7 @@
 
     weight_sum = Scatter(place, piece_of(packed), *sum_scatter)
     weight_sum.start()
-    align[...] = three(nt, both[:, : 2 * width], w_cat[...])
+    align[...] = three(nn, both[:, : 2 * width], w_cat)
     weight_sum.pair()
     weight_sum.cross()
     weight_sum.finish()
@@ -420,14 +430,18 @@
     spread.pair()
     spread.finish()
 
+
+def unpack_kernel(align, total_sum, align_out, left_w, right_w, out_w):
+    width, depth = left_w.shape
+    base = width * width
+    align_out[...] = align[...]
     for c in range(width):
         out_w[pl.ds(c, width, stride=width), :] = total_sum[c * width : (c + 1) * width, :]
-    for t in range(tiles):
+    for t in range(depth // LANES):
         at = slice(t * LANES, (t + 1) * LANES)
-        part = total_sum[base + t * 2 * width : base + (t + 1) * 2 * width, :]
-        part = jnp.concatenate([part, jnp.zeros((LANES - 2 * width, LANES), F32)], axis=0).T
-        left_w[at, :] = part[:, :width]
-        right_w[at, :] = part[:, width : 2 * width]
+        first = base + t * 2 * width
+        left_w[:, at] = total_sum[first : first + width, :]
+        right_w[:, at] = total_sum[first + width : first + 2 * width, :]
 
 
 def local(n, act, valid, flags, w_left, w_right, w_final, cdd):
@@ -435,24 +449,20 @@
     fam, _, depth = act.shape
     width = w_left.shape[1]
     feats = width * fam
-    keep_t = valid.astype(F32).T
-    present = flags.astype(F32)
-    marks = jnp.concatenate([keep_t, present[:, None], jnp.zeros((rows, LANES - fam - 1), F32)], axis=1)
     step = min(4, rows)
-    keep_rows = jnp.concatenate([keep_t, jnp.zeros((rows, LANES - fam), F32)], axis=1).reshape(-1, step, LANES)
     used = width * width + 2 * depth * width // LANES
     piece = -(-used // (8 * n)) * 8
     vm = pl.BlockSpec(memory_space=pltpu.VMEM)
     f32 = lambda *shape: pltpu.VMEM(shape, F32)
     b16 = lambda *shape: pltpu.VMEM(shape, BF16)
-    align, left_w, right_w, out_w = pl.pallas_call(
+    align, total_sum = pl.pallas_call(
         functools.partial(kernel, n, step, fam),
         out_shape=tuple(
             jax.ShapeDtypeStruct(shape, F32)
-            for shape in ((fam * rows, depth), (depth, width), (depth, width), (width * width, pair))
+            for shape in ((fam * rows, depth), (n * piece, LANES))
         ),
-        in_specs=[vm] * 7 + [pl.BlockSpec(memory_space=pl.ANY)],
-        out_specs=(vm,) * 4,
+        in_specs=[vm] * 6 + [pl.BlockSpec(memory_space=pl.ANY)],
+        out_specs=(vm,) * 2,
         scratch_shapes=[
             f32(rows, total, pair),
             f32(rows, feats, pair),
@@ -473,7 +483,10 @@
             f32(rows * fam, LANES),
             f32(fam * rows, LANES),
             f32(n * piece, LANES),
-            f32(n * piece, LANES),
+            f32(LANES, LANES),
+            f32(rows, LANES),
+            f32(rows // step, step, LANES),
+            f32(rows // step, 1, step),
             pltpu.SemaphoreType.DMA((rows // step,)),
         ]
         + gather_sems(n) * 3
@@ -483,15 +496,24 @@
         compiler_params=pltpu.CompilerParams(collective_id=0, has_side_effects=True, vmem_limit_bytes=60 << 20),
     )(
         act.reshape(fam * rows, depth),
-        keep_t,
-        marks,
-        keep_rows,
-        present.reshape(-1, 1, step),
-        jnp.concatenate([w_left, w_right], axis=1),
+        valid,
+        flags.reshape(1, rows),
+        w_left.T,
+        w_right.T,
         w_final,
         cdd,
     )
-    return align.reshape(fam, rows, depth), left_w, right_w, out_w
+    align, left_w, right_w, out_w = pl.pallas_call(
+        unpack_kernel,
+        out_shape=tuple(
+            jax.ShapeDtypeStruct(shape, F32)
+            for shape in ((fam * rows, depth), (width, depth), (width, depth), (width * width, pair))
+        ),
+        in_specs=[vm] * 2,
+        out_specs=(vm,) * 4,
+        name="unpack",
+    )(align, total_sum)
+    return align.reshape(fam, rows, depth), left_w.T, right_w.T, out_w
 
 
 def solution(mesh):

time: 84.8 us -> 74.1 us (0.87)
  local copies, waits for them, and re-layouts: 9.56 us -> 0 us
  other arithmetic: 2.8 us -> 0 us
  Pallas kernels: 71.3 us -> 73.3 us
    unnamed x8 -> x0, local copies, waits for them, and re-layouts: 8.65 us -> none
    pallas_call x0 -> x1, Pallas kernels: none -> 2.54 us  [local(): pl.pallas_call(unpack_kernel, out_shape=tuple((jax.ShapeDtypeStruct(shape...]
    concatenate x2 -> x0, other arithmetic: 1.45 us -> none  [the longest x1 0.76 us: local(): jnp.concatenate([w_left, w_right], axis=1)]
    convert_element_type x2 -> x0, other arithmetic: 1.36 us -> none  [the longest x1 0.7 us: local(): keep_t = valid.astype(F32).T]
where the time goes in v3:
time: 74.1 us; the launch traced here: 73.9 us
  Pallas kernels  73.3 us (99%)
    pallas_call x1, Pallas kernels, local(): pl.pallas_call(functools.partial(kernel, n, step, fam), out_shape=tuple((...  70.8 us
    pallas_call x1, Pallas kernels, local(): pl.pallas_call(unpack_kernel, out_shape=tuple((jax.ShapeDtypeStruct(shape...  2.54 us

profile of v3, /device:TPU:0, one launch (start us, length us, event | category | flops | bytes accessed | tf_op | source)
XLA Modules:
  0.0 73.9 jit_solution(16906232152647681818)
XLA Ops:
  0.6 70.8 %outer_mean_grad.1 = (f32[512,256]{1,0:T(8,128)}, f32[1152,128]{1,0:T(8,128)}) custom-call(f32[512,256]{1,0:T(8,128)} %bitcast.7, s32[16,32]{1,0:T(8,128)} %valid.1, s32[1,32]{1,0:T(1,128)} %bitcast.10, f32[32,256]{1,0:T(8,128)} %bitcast.8, f32[32,256]{1,0:T(8,128)} %bitcast.9, f32[1024,128]{1,0:T(8,128)} %w_final.1, f32[32,512,128]{2,1,0:T(8,128)} %cdd_hbm.1), custom_call_target="tpu_custom_call" | custom-call | tf_op jit(solution)/shard_map/outer_mean_grad/pallas_call | solution.py:458
  71.4 2.5 %unpack.1 = (f32[512,256]{1,0:T(8,128)}, f32[32,256]{1,0:T(8,128)}, f32[32,256]{1,0:T(8,128)}, f32[1024,128]{1,0:T(8,128)}) custom-call(f32[512,256]{1,0:T(8,128)} %get-tuple-element.10.align, f32[1152,128]{1,0:T(8,128)} %get-tuple-element.11.total_sum), custom_call_target="tpu_custom_call" | custom-call | tf_op jit(solution)/shard_map/unpack/pallas_call | solution.py:506
